TPU v7x, 32 devices: a whole 2x2x4 slice. The times are simulated.
32 devices in a mesh: chain: 8 (over z, y), col: 4 (over x, core).
Axes of the slice: x: 2, y: 2, z: 4, core: 2. Of those that a mesh axis runs over, the one named last changes fastest.
Arguments:
- rhs: bfloat16 [4, 8, 32, 128], P(None, 'chain'), may hold values from -6 to 6
- pattern: int32 [4, 8, 24], P(None, 'chain', 'col'), may hold values from 0 to 31, as said below
- factor: bfloat16 [4, 8, 24, 128, 128], P(None, 'chain', 'col'), may hold values from -0.1875 to 0.1875
- inverse: bfloat16 [4, 8, 128, 128], P(None, 'chain'), as said below
- level_size: int32 [6], replicated, may hold values from 1 to 8, 32 in all
Outputs:
- half_solved: bfloat16 [4, 8, 32, 128], P(None, 'chain')
- solved: bfloat16 [4, 8, 32, 128], P(None, 'chain')
Inputs may be any that keep to these rules, and one draw needn't show every extreme that they name: Among the pattern entries held by one index of chain and one index of col (all 4 of its block rows), at most 3 name block rows on any one index of chain (block row mod 8); in every such group exactly 3 name block rows on one index of chain that is common to all groups of that index of col. A block row may name a block row more than once. `inverse`: each block is lower triangular with a diagonal between 0.3 and 2.
All inputs are finite; a program needn't handle non-finite values.
Results may differ from a plain program's by a relative error of at most 0.013.
Values may be sent and summed in bfloat16 or wider, within the bound.
A program may use at most 64 MiB of HBM per device.

v0:
```python
import jax
import jax.numpy as jnp
from jax import lax
from jax.sharding import PartitionSpec as P


def level_index(positions, ends):
    return jnp.sum((positions[..., None] >= ends).astype(jnp.int32), axis=-1)


def per_device(rhs, pattern, factor, inverse, level_size):
    lane_count = lax.axis_size("chain")
    chain_pos = lax.axis_index("chain")
    row_count = rhs.shape[0]
    probe_count = rhs.shape[2]
    width = rhs.shape[3]
    entries = pattern.shape[2]
    level_count = level_size.shape[0]
    total = row_count * lane_count
    ends = jnp.cumsum(level_size)
    starts = ends - level_size
    own_rows = jnp.arange(row_count, dtype=jnp.int32) * lane_count + chain_pos
    own_level = level_index(own_rows, ends)
    columns = pattern[:, 0, :]
    column_level = level_index(columns, ends)
    keep = column_level < own_level[:, None]
    blocks = factor[:, 0]
    inverse_rows = inverse[:, 0]
    right = rhs[:, 0]
    slot_ids = jnp.arange(row_count, dtype=jnp.int32)
    lane_ids = jnp.arange(lane_count, dtype=jnp.int32)

    def locate(level):
        picked = own_level == level
        own_slot = jnp.sum(jnp.where(picked, slot_ids, 0))
        return (picked, own_slot, jnp.any(picked))

    def forward_level(level, carry):
        store, half_local = carry
        picked, own_slot, is_live = locate(level)
        wanted = keep[own_slot] & is_live
        chosen = jnp.where(
            wanted[:, None, None], store[columns[own_slot]], jnp.zeros((), jnp.bfloat16)
        )
        partial_value = jnp.einsum(
            "jpb,jcb->pc", chosen, blocks[own_slot], preferred_element_type=jnp.float32
        )
        summed = lax.psum(partial_value, "col")
        rest = (right[own_slot].astype(jnp.float32) - summed).astype(jnp.bfloat16)
        segment = jnp.dot(
            rest, inverse_rows[own_slot].T, preferred_element_type=jnp.float32
        ).astype(jnp.bfloat16)
        segment = jnp.where(is_live, segment, jnp.zeros((), jnp.bfloat16))
        front = lax.all_gather(segment[None], "chain", axis=0, tiled=True)
        half_local = jnp.where(picked[:, None, None], segment[None], half_local)
        start = starts[level]
        ordered = front[(start + lane_ids) % lane_count]
        store = lax.dynamic_update_slice_in_dim(store, ordered, start, 0)
        return (store, half_local)

    store = jnp.zeros((total + lane_count, probe_count, width), jnp.bfloat16)
    half_local = jnp.zeros((row_count, probe_count, width), jnp.bfloat16)
    store, half_local = lax.fori_loop(0, level_count, forward_level, (store, half_local))
    solved_local = jnp.zeros((row_count, probe_count, width), jnp.bfloat16)
    count = row_count * entries
    capacity = max(2, (count + lane_count - 1) // lane_count)
    slots_all = lane_count * capacity
    flat_cols = columns.reshape(count)
    flat_src = jnp.broadcast_to(own_rows[:, None], (row_count, entries)).reshape(count)
    dest = flat_cols % lane_count
    onehot = (dest[:, None] == lane_ids[None, :]).astype(jnp.int32)
    before = jnp.cumsum(onehot, axis=0) - onehot
    rank = jnp.sum(before * onehot, axis=1)
    slot = dest * capacity + rank
    select = slot[None, :] == jnp.arange(slots_all, dtype=jnp.int32)[:, None]
    sent_blocks = jnp.dot(
        select.astype(jnp.bfloat16),
        blocks.reshape(count, width * width),
        preferred_element_type=jnp.float32,
    )
    sent_blocks = sent_blocks.astype(jnp.bfloat16).reshape(lane_count, capacity, width, width)
    sent_src = jnp.sum(jnp.where(select, flat_src[None, :] + 1, 0), axis=1) - 1
    sent_dst = jnp.sum(jnp.where(select, flat_cols[None, :] + 1, 0), axis=1) - 1
    sent_meta = jnp.stack([sent_src, sent_dst], axis=1).reshape(lane_count, capacity, 2)
    home_blocks, home_meta = (
        lax.all_to_all(sent_blocks, "chain", split_axis=0, concat_axis=0, tiled=True),
        lax.all_to_all(sent_meta, "chain", split_axis=0, concat_axis=0, tiled=True),
    )
    home_blocks = home_blocks.reshape(slots_all, width, width)
    home_meta = home_meta.reshape(slots_all, 2)
    source_row = home_meta[:, 0]
    target_row = home_meta[:, 1]
    valid = source_row >= 0
    source_level = level_index(source_row, ends)
    target_level = level_index(target_row, ends)
    home_keep = valid & (target_level < source_level)
    source_lane = jnp.where(valid, source_row % lane_count, 0)
    home_slot = jnp.where(valid, target_row // lane_count, -1)

    def home_level(counter, carry):
        accum, solved_now = carry
        level = level_count - 1 - counter
        picked, own_slot, is_live = locate(level)
        summed = lax.psum(accum[own_slot], "col")
        rest = (half_local[own_slot].astype(jnp.float32) - summed).astype(jnp.bfloat16)
        segment = jnp.dot(rest, inverse_rows[own_slot], preferred_element_type=jnp.float32).astype(
            jnp.bfloat16
        )
        segment = jnp.where(is_live, segment, jnp.zeros((), jnp.bfloat16))
        solved_now = jnp.where(picked[:, None, None], segment[None], solved_now)
        front = lax.all_gather(segment[None], "chain", axis=0, tiled=True)
        active = home_keep & (source_level == level)
        incoming = front[source_lane]
        terms = jnp.einsum(
            "kpc,kcb->kpb", incoming, home_blocks, preferred_element_type=jnp.float32
        )
        spread = ((home_slot[None, :] == slot_ids[:, None]) & active[None, :]).astype(jnp.float32)
        added = jnp.dot(
            spread,
            terms.reshape(slots_all, probe_count * width),
            precision=lax.Precision.HIGHEST,
            preferred_element_type=jnp.float32,
        )
        accum = accum + added.reshape(row_count, probe_count, width)
        return (accum, solved_now)

    accum = jnp.zeros((row_count, probe_count, width), jnp.float32)
    accum, solved_local = lax.fori_loop(0, level_count, home_level, (accum, solved_local))
    return (half_local[:, None], solved_local[:, None])


def solution(mesh):
    return jax.shard_map(
        per_device,
        mesh=mesh,
        in_specs=(
            P(None, "chain", None, None),
            P(None, "chain", "col"),
            P(None, "chain", "col", None, None),
            P(None, "chain", None, None),
            P(),
        ),
        out_specs=(P(None, "chain", None, None), P(None, "chain", None, None)),
        check_vma=False,
    )
```

profile of v0, /device:TPU:0, one launch (start us, length us, event | category | flops | bytes accessed | tf_op | source)
XLA Modules:
  0.0 617.3 jit_solution(10101479652952594900)
XLA Ops:
  23.2 314.8 %while.35 = (s32[]{:T(128)}, bf16[40,32,128]{2,1,0:T(8,128)(2,1)S(1)}, bf16[4,32,128]{2,1,0:T(8,128)(2,1)S(1)}, s32[4]{0:T(128)S(1)}, bf16[4,32,128]{2,1,0:T(8,1...) while((s32[]{:T(128)}, ...), condition=%wide.region_7.8_spmd.clone, body=%wide.region_3.7_spmd.clone.sunk | while | flops 7424167 | bytes 878571 | solution.py:63
  29.5 10.4 %psum.30 = f32[32,128]{1,0:T(8,128)S(1)} all-reduce(f32[32,128]{1,0:T(8,128)S(1)} %convolution_bitcast_fusion.2), channel_id=1, replica_groups=mesh['chain'=8,'col'=4] {'col'}, use_global_device_ids=true, to_apply=%region_6.6 | all-reduce | flops 4096 | bytes 32768 | tf_op jit(solution)/shard_map/while/body/eval_jaxpr/psum | solution.py:48
  41.4 31.1 %all-gather.6 = bf16[256,128]{1,0:T(8,128)(2,1)S(1)} all-gather(bf16[32,128]{1,0:T(8,128)(2,1)S(1)} %fusion.84), channel_id=2, replica_groups=mesh['chain'=8,'col'=4] {'chain'}, dimensions={0}, use_global_device_ids=true | all-gather | bytes 73728 | tf_op jit(solution)/shard_map/while/body/eval_jaxpr/all_gather | solution.py:54
  82.6 10.1 %psum.30 = f32[32,128]{1,0:T(8,128)S(1)} all-reduce(f32[32,128]{1,0:T(8,128)S(1)} %convolution_bitcast_fusion.2), channel_id=1, replica_groups=mesh['chain'=8,'col'=4] {'col'}, use_global_device_ids=true, to_apply=%region_6.6 | all-reduce | flops 4096 | bytes 32768 | tf_op jit(solution)/shard_map/while/body/eval_jaxpr/psum | solution.py:48
  94.2 30.6 %all-gather.6 = bf16[256,128]{1,0:T(8,128)(2,1)S(1)} all-gather(bf16[32,128]{1,0:T(8,128)(2,1)S(1)} %fusion.84), channel_id=2, replica_groups=mesh['chain'=8,'col'=4] {'chain'}, dimensions={0}, use_global_device_ids=true | all-gather | bytes 73728 | tf_op jit(solution)/shard_map/while/body/eval_jaxpr/all_gather | solution.py:54
  135.0 10.1 %psum.30 = f32[32,128]{1,0:T(8,128)S(1)} all-reduce(f32[32,128]{1,0:T(8,128)S(1)} %convolution_bitcast_fusion.2), channel_id=1, replica_groups=mesh['chain'=8,'col'=4] {'col'}, use_global_device_ids=true, to_apply=%region_6.6 | all-reduce | flops 4096 | bytes 32768 | tf_op jit(solution)/shard_map/while/body/eval_jaxpr/psum | solution.py:48
  146.6 30.6 %all-gather.6 = bf16[256,128]{1,0:T(8,128)(2,1)S(1)} all-gather(bf16[32,128]{1,0:T(8,128)(2,1)S(1)} %fusion.84), channel_id=2, replica_groups=mesh['chain'=8,'col'=4] {'chain'}, dimensions={0}, use_global_device_ids=true | all-gather | bytes 73728 | tf_op jit(solution)/shard_map/while/body/eval_jaxpr/all_gather | solution.py:54
  187.3 10.1 %psum.30 = f32[32,128]{1,0:T(8,128)S(1)} all-reduce(f32[32,128]{1,0:T(8,128)S(1)} %convolution_bitcast_fusion.2), channel_id=1, replica_groups=mesh['chain'=8,'col'=4] {'col'}, use_global_device_ids=true, to_apply=%region_6.6 | all-reduce | flops 4096 | bytes 32768 | tf_op jit(solution)/shard_map/while/body/eval_jaxpr/psum | solution.py:48
  198.9 30.6 %all-gather.6 = bf16[256,128]{1,0:T(8,128)(2,1)S(1)} all-gather(bf16[32,128]{1,0:T(8,128)(2,1)S(1)} %fusion.84), channel_id=2, replica_groups=mesh['chain'=8,'col'=4] {'chain'}, dimensions={0}, use_global_device_ids=true | all-gather | bytes 73728 | tf_op jit(solution)/shard_map/while/body/eval_jaxpr/all_gather | solution.py:54
  239.6 10.1 %psum.30 = f32[32,128]{1,0:T(8,128)S(1)} all-reduce(f32[32,128]{1,0:T(8,128)S(1)} %convolution_bitcast_fusion.2), channel_id=1, replica_groups=mesh['chain'=8,'col'=4] {'col'}, use_global_device_ids=true, to_apply=%region_6.6 | all-reduce | flops 4096 | bytes 32768 | tf_op jit(solution)/shard_map/while/body/eval_jaxpr/psum | solution.py:48
  251.2 30.6 %all-gather.6 = bf16[256,128]{1,0:T(8,128)(2,1)S(1)} all-gather(bf16[32,128]{1,0:T(8,128)(2,1)S(1)} %fusion.84), channel_id=2, replica_groups=mesh['chain'=8,'col'=4] {'chain'}, dimensions={0}, use_global_device_ids=true | all-gather | bytes 73728 | tf_op jit(solution)/shard_map/while/body/eval_jaxpr/all_gather | solution.py:54
  291.9 10.1 %psum.30 = f32[32,128]{1,0:T(8,128)S(1)} all-reduce(f32[32,128]{1,0:T(8,128)S(1)} %convolution_bitcast_fusion.2), channel_id=1, replica_groups=mesh['chain'=8,'col'=4] {'col'}, use_global_device_ids=true, to_apply=%region_6.6 | all-reduce | flops 4096 | bytes 32768 | tf_op jit(solution)/shard_map/while/body/eval_jaxpr/psum | solution.py:48
  303.6 30.6 %all-gather.6 = bf16[256,128]{1,0:T(8,128)(2,1)S(1)} all-gather(bf16[32,128]{1,0:T(8,128)(2,1)S(1)} %fusion.84), channel_id=2, replica_groups=mesh['chain'=8,'col'=4] {'chain'}, dimensions={0}, use_global_device_ids=true | all-gather | bytes 73728 | tf_op jit(solution)/shard_map/while/body/eval_jaxpr/all_gather | solution.py:54
  338.2 278.4 %while.36 = (s32[]{:T(128)}, f32[4,32,128]{2,0,1:T(4,128)S(1)}, bf16[4,32,128]{2,1,0:T(8,128)(2,1)S(1)}, s32[24]{0:T(128)S(1)}, s32[24]{0:T(128)S(1)}, /*index=5...) while((s32[]{:T(128)}, f32[4,32,128]{2,0,1:T(4,128)S(1)}, ...), condition=%wide.region_18.19_spmd.clone.clone, body=%wide.region_14.18_spmd.clone.clone.sunk | while | flops 31024460 | bytes 2709372 | solution.py:128
  341.7 10.1 %psum.31 = f32[32,128]{1,0:T(8,128)S(1)} all-reduce(f32[32,128]{1,0:T(8,128)S(1)} %bitcast.150), channel_id=1, replica_groups=mesh['chain'=8,'col'=4] {'col'}, use_global_device_ids=true, to_apply=%region_17.17 | all-reduce | flops 4096 | bytes 32768 | tf_op jit(solution)/shard_map/while/body/eval_jaxpr/psum | solution.py:104
  352.6 30.5 %all-gather.7 = bf16[256,128]{1,0:T(8,128)(2,1)S(1)} all-gather(bf16[32,128]{1,0:T(8,128)(2,1)S(1)} %fusion.94), channel_id=3, replica_groups=mesh['chain'=8,'col'=4] {'chain'}, dimensions={0}, use_global_device_ids=true | all-gather | bytes 73728 | tf_op jit(solution)/shard_map/while/body/eval_jaxpr/all_gather | solution.py:111
  388.1 10.1 %psum.31 = f32[32,128]{1,0:T(8,128)S(1)} all-reduce(f32[32,128]{1,0:T(8,128)S(1)} %bitcast.150), channel_id=1, replica_groups=mesh['chain'=8,'col'=4] {'col'}, use_global_device_ids=true, to_apply=%region_17.17 | all-reduce | flops 4096 | bytes 32768 | tf_op jit(solution)/shard_map/while/body/eval_jaxpr/psum | solution.py:104
  399.0 30.5 %all-gather.7 = bf16[256,128]{1,0:T(8,128)(2,1)S(1)} all-gather(bf16[32,128]{1,0:T(8,128)(2,1)S(1)} %fusion.94), channel_id=3, replica_groups=mesh['chain'=8,'col'=4] {'chain'}, dimensions={0}, use_global_device_ids=true | all-gather | bytes 73728 | tf_op jit(solution)/shard_map/while/body/eval_jaxpr/all_gather | solution.py:111
  434.5 10.1 %psum.31 = f32[32,128]{1,0:T(8,128)S(1)} all-reduce(f32[32,128]{1,0:T(8,128)S(1)} %bitcast.150), channel_id=1, replica_groups=mesh['chain'=8,'col'=4] {'col'}, use_global_device_ids=true, to_apply=%region_17.17 | all-reduce | flops 4096 | bytes 32768 | tf_op jit(solution)/shard_map/while/body/eval_jaxpr/psum | solution.py:104
  445.4 30.5 %all-gather.7 = bf16[256,128]{1,0:T(8,128)(2,1)S(1)} all-gather(bf16[32,128]{1,0:T(8,128)(2,1)S(1)} %fusion.94), channel_id=3, replica_groups=mesh['chain'=8,'col'=4] {'chain'}, dimensions={0}, use_global_device_ids=true | all-gather | bytes 73728 | tf_op jit(solution)/shard_map/while/body/eval_jaxpr/all_gather | solution.py:111
  480.9 10.1 %psum.31 = f32[32,128]{1,0:T(8,128)S(1)} all-reduce(f32[32,128]{1,0:T(8,128)S(1)} %bitcast.150), channel_id=1, replica_groups=mesh['chain'=8,'col'=4] {'col'}, use_global_device_ids=true, to_apply=%region_17.17 | all-reduce | flops 4096 | bytes 32768 | tf_op jit(solution)/shard_map/while/body/eval_jaxpr/psum | solution.py:104
  491.8 30.5 %all-gather.7 = bf16[256,128]{1,0:T(8,128)(2,1)S(1)} all-gather(bf16[32,128]{1,0:T(8,128)(2,1)S(1)} %fusion.94), channel_id=3, replica_groups=mesh['chain'=8,'col'=4] {'chain'}, dimensions={0}, use_global_device_ids=true | all-gather | bytes 73728 | tf_op jit(solution)/shard_map/while/body/eval_jaxpr/all_gather | solution.py:111
  538.2 30.5 %all-gather.7 = bf16[256,128]{1,0:T(8,128)(2,1)S(1)} all-gather(bf16[32,128]{1,0:T(8,128)(2,1)S(1)} %fusion.94), channel_id=3, replica_groups=mesh['chain'=8,'col'=4] {'chain'}, dimensions={0}, use_global_device_ids=true | all-gather | bytes 73728 | tf_op jit(solution)/shard_map/while/body/eval_jaxpr/all_gather | solution.py:111
  584.6 30.5 %all-gather.7 = bf16[256,128]{1,0:T(8,128)(2,1)S(1)} all-gather(bf16[32,128]{1,0:T(8,128)(2,1)S(1)} %fusion.94), channel_id=3, replica_groups=mesh['chain'=8,'col'=4] {'chain'}, dimensions={0}, use_global_device_ids=true | all-gather | bytes 73728 | tf_op jit(solution)/shard_map/while/body/eval_jaxpr/all_gather | solution.py:111
  (205 shorter events, 111.8 us)
Async XLA Ops:
  4.0 13.8 %all-to-all-start = ((s32[8,3,2]{1,2,0:T(2,128)}), s32[8,3,2]{1,2,0:T(2,128)S(1)}, u32[]{:S(2)}, u32[]{:S(2)}) async-start(s32[8,3,2]{1,2,0:T(2,128)} %copy.16), calls=%async_computation | async-start | bytes 16384 | tf_op jit(solution)/shard_map/all_to_all | solution.py:87
  17.8 5.3 copy-start.2
  17.8 320.4 %all-to-all-start.1 = ((bf16[8,3,128,128]{3,2,1,0:T(8,128)(2,1)}), bf16[8,3,128,128]{3,2,1,0:T(8,128)(2,1)S(1)}, u32[]{:S(2)}, u32[]{:S(2)}) async-start(bf16[8,3,128,128]{3,2,1,0:T(8,128)(2,1)} %bitcast.42), calls=%async_computation.1 | async-start | bytes 1572864 | tf_op jit(solution)/shard_map/all_to_all | solution.py:86
  616.6 0.6 copy-start
  616.6 0.6 copy-start.1
where the time goes:
time: 619 us; the launch traced here: 617 us
  blocking collectives  489 us (79%)
  loops' own time  36 us (6%)
  other arithmetic  33.2 us (5%)
  matrix products  26.7 us (4%)
  local copies, waits for them, and re-layouts  18.2 us (3%)
  starting transfers between devices  12.6 us (2%)
    all_gather x6, blocking collectives, forward_level(): front = lax.all_gather(segment[None], 'chain', axis=0, tiled=True)  184 us
    all_gather x6, blocking collectives, home_level(): front = lax.all_gather(segment[None], 'chain', axis=0, tiled=True)  183 us
    psum x6, blocking collectives, forward_level(): summed = lax.psum(partial_value, 'col')  61.1 us
    psum x6, blocking collectives, home_level(): summed = lax.psum(accum[own_slot], 'col')  60.7 us
    another operation x1, loops' own time, per_device(): lax.fori_loop(0, level_count, forward_level, (store, half_local))  23.3 us
    another operation x1, loops' own time, per_device(): lax.fori_loop(0, level_count, home_level, (accum, solved_local))  12.7 us
  transfers between devices with their start and end apart: 2, of which 1 were waited for; matrix products, arithmetic and copies ran while one was open for 8% of the time, Pallas kernels for 0%

commit v1 on v0

--- a/solution.py
+++ b/solution.py
@@ -1,7 +1,16 @@
+import functools
 import jax
 import jax.numpy as jnp
 from jax import lax
 from jax.sharding import PartitionSpec as P
+from jax.lax import all_gather
+
+
+def compute_rings(page, row_axis):
+    return jnp.sum(all_gather(page, axis_name=row_axis), 0)
+
+
+turn_panels = functools.partial(compute_rings, row_axis="col")
 
 
 def level_index(positions, ends):
@@ -101,7 +110,7 @@
         accum, solved_now = carry
         level = level_count - 1 - counter
         picked, own_slot, is_live = locate(level)
-        summed = lax.psum(accum[own_slot], "col")
+        summed = turn_panels(accum[own_slot])
         rest = (half_local[own_slot].astype(jnp.float32) - summed).astype(jnp.bfloat16)
         segment = jnp.dot(rest, inverse_rows[own_slot], preferred_element_type=jnp.float32).astype(
             jnp.bfloat16

time: 619 us -> 590 us (0.953)
  blocking collectives: 489 us -> 460 us
    psum x6 -> x0, blocking collectives: 60.7 us -> none  [home_level(): summed = lax.psum(accum[own_slot], 'col')]
    all_gather x0 -> x6, blocking collectives: none -> 31.4 us  [compute_rings(): return jnp.sum(all_gather(page, axis_name=row_axis), 0)]
  transfers between devices with their start and end apart: 2 -> 2, of which waited for: 1 -> 1; matrix products, arithmetic and copies ran while one was open for 8% -> 9% of each run, Pallas kernels for 0% -> 0%
where the time goes in v1:
time: 590 us; the launch traced here: 588 us
  blocking collectives  460 us (78%)
  loops' own time  36 us (6%)
  other arithmetic  33.3 us (6%)
  matrix products  26.7 us (5%)
  local copies, waits for them, and re-layouts  18.2 us (3%)
  starting transfers between devices  12.6 us (2%)
    all_gather x6, blocking collectives, forward_level(): front = lax.all_gather(segment[None], 'chain', axis=0, tiled=True)  184 us
    all_gather x6, blocking collectives, home_level(): front = lax.all_gather(segment[None], 'chain', axis=0, tiled=True)  183 us
    psum x6, blocking collectives, forward_level(): summed = lax.psum(partial_value, 'col')  61.1 us
    all_gather x6, blocking collectives, compute_rings(): return jnp.sum(all_gather(page, axis_name=row_axis), 0)  31.4 us
    another operation x1, loops' own time, per_device(): lax.fori_loop(0, level_count, forward_level, (store, half_local))  23.3 us
    another operation x1, loops' own time, per_device(): lax.fori_loop(0, level_count, home_level, (accum, solved_local))  12.7 us
  transfers between devices with their start and end apart: 2, of which 1 were waited for; matrix products, arithmetic and copies ran while one was open for 9% of the time, Pallas kernels for 0%

profile of v1, /device:TPU:0, one launch (start us, length us, event | category | flops | bytes accessed | tf_op | source)
XLA Modules:
  0.0 588.0 jit_solution(14926145971442606721)
XLA Ops:
  4.0 7.3 %all-to-all-start = ((s32[8,3,2]{1,2,0:T(2,128)}), s32[8,3,2]{1,2,0:T(2,128)S(1)}, u32[]{:S(2)}, u32[]{:S(2)}) async-start(s32[8,3,2]{1,2,0:T(2,128)} %copy.18), calls=%async_computation | async-start | bytes 16384 | tf_op jit(solution)/shard_map/all_to_all | solution.py:96
  17.8 5.3 all-to-all-start.1
  23.2 314.8 %while.35 = (s32[]{:T(128)}, bf16[40,32,128]{2,1,0:T(8,128)(2,1)S(1)}, bf16[4,32,128]{2,1,0:T(8,128)(2,1)S(1)}, s32[4]{0:T(128)S(1)}, bf16[4,32,128]{2,1,0:T(8,1...) while((s32[]{:T(128)}, ...), condition=%wide.region_7.8_spmd.clone, body=%wide.region_3.7_spmd.clone.sunk | while | flops 7424167 | bytes 878571 | solution.py:72
  29.5 10.4 %psum.16 = f32[32,128]{1,0:T(8,128)S(1)} all-reduce(f32[32,128]{1,0:T(8,128)S(1)} %convolution_bitcast_fusion.2), channel_id=1, replica_groups=mesh['chain'=8,'col'=4] {'col'}, use_global_device_ids=true, to_apply=%region_6.6 | all-reduce | flops 4096 | bytes 32768 | tf_op jit(solution)/shard_map/while/body/eval_jaxpr/psum | solution.py:57
  41.4 31.1 %all-gather.6 = bf16[256,128]{1,0:T(8,128)(2,1)S(1)} all-gather(bf16[32,128]{1,0:T(8,128)(2,1)S(1)} %fusion.84), channel_id=2, replica_groups=mesh['chain'=8,'col'=4] {'chain'}, dimensions={0}, use_global_device_ids=true | all-gather | bytes 73728 | tf_op jit(solution)/shard_map/while/body/eval_jaxpr/all_gather | solution.py:63
  82.6 10.1 %psum.16 = f32[32,128]{1,0:T(8,128)S(1)} all-reduce(f32[32,128]{1,0:T(8,128)S(1)} %convolution_bitcast_fusion.2), channel_id=1, replica_groups=mesh['chain'=8,'col'=4] {'col'}, use_global_device_ids=true, to_apply=%region_6.6 | all-reduce | flops 4096 | bytes 32768 | tf_op jit(solution)/shard_map/while/body/eval_jaxpr/psum | solution.py:57
  94.2 30.6 %all-gather.6 = bf16[256,128]{1,0:T(8,128)(2,1)S(1)} all-gather(bf16[32,128]{1,0:T(8,128)(2,1)S(1)} %fusion.84), channel_id=2, replica_groups=mesh['chain'=8,'col'=4] {'chain'}, dimensions={0}, use_global_device_ids=true | all-gather | bytes 73728 | tf_op jit(solution)/shard_map/while/body/eval_jaxpr/all_gather | solution.py:63
  135.0 10.1 %psum.16 = f32[32,128]{1,0:T(8,128)S(1)} all-reduce(f32[32,128]{1,0:T(8,128)S(1)} %convolution_bitcast_fusion.2), channel_id=1, replica_groups=mesh['chain'=8,'col'=4] {'col'}, use_global_device_ids=true, to_apply=%region_6.6 | all-reduce | flops 4096 | bytes 32768 | tf_op jit(solution)/shard_map/while/body/eval_jaxpr/psum | solution.py:57
  146.6 30.6 %all-gather.6 = bf16[256,128]{1,0:T(8,128)(2,1)S(1)} all-gather(bf16[32,128]{1,0:T(8,128)(2,1)S(1)} %fusion.84), channel_id=2, replica_groups=mesh['chain'=8,'col'=4] {'chain'}, dimensions={0}, use_global_device_ids=true | all-gather | bytes 73728 | tf_op jit(solution)/shard_map/while/body/eval_jaxpr/all_gather | solution.py:63
  187.3 10.1 %psum.16 = f32[32,128]{1,0:T(8,128)S(1)} all-reduce(f32[32,128]{1,0:T(8,128)S(1)} %convolution_bitcast_fusion.2), channel_id=1, replica_groups=mesh['chain'=8,'col'=4] {'col'}, use_global_device_ids=true, to_apply=%region_6.6 | all-reduce | flops 4096 | bytes 32768 | tf_op jit(solution)/shard_map/while/body/eval_jaxpr/psum | solution.py:57
  198.9 30.6 %all-gather.6 = bf16[256,128]{1,0:T(8,128)(2,1)S(1)} all-gather(bf16[32,128]{1,0:T(8,128)(2,1)S(1)} %fusion.84), channel_id=2, replica_groups=mesh['chain'=8,'col'=4] {'chain'}, dimensions={0}, use_global_device_ids=true | all-gather | bytes 73728 | tf_op jit(solution)/shard_map/while/body/eval_jaxpr/all_gather | solution.py:63
  239.6 10.1 %psum.16 = f32[32,128]{1,0:T(8,128)S(1)} all-reduce(f32[32,128]{1,0:T(8,128)S(1)} %convolution_bitcast_fusion.2), channel_id=1, replica_groups=mesh['chain'=8,'col'=4] {'col'}, use_global_device_ids=true, to_apply=%region_6.6 | all-reduce | flops 4096 | bytes 32768 | tf_op jit(solution)/shard_map/while/body/eval_jaxpr/psum | solution.py:57
  251.2 30.6 %all-gather.6 = bf16[256,128]{1,0:T(8,128)(2,1)S(1)} all-gather(bf16[32,128]{1,0:T(8,128)(2,1)S(1)} %fusion.84), channel_id=2, replica_groups=mesh['chain'=8,'col'=4] {'chain'}, dimensions={0}, use_global_device_ids=true | all-gather | bytes 73728 | tf_op jit(solution)/shard_map/while/body/eval_jaxpr/all_gather | solution.py:63
  291.9 10.1 %psum.16 = f32[32,128]{1,0:T(8,128)S(1)} all-reduce(f32[32,128]{1,0:T(8,128)S(1)} %convolution_bitcast_fusion.2), channel_id=1, replica_groups=mesh['chain'=8,'col'=4] {'col'}, use_global_device_ids=true, to_apply=%region_6.6 | all-reduce | flops 4096 | bytes 32768 | tf_op jit(solution)/shard_map/while/body/eval_jaxpr/psum | solution.py:57
  303.6 30.6 %all-gather.6 = bf16[256,128]{1,0:T(8,128)(2,1)S(1)} all-gather(bf16[32,128]{1,0:T(8,128)(2,1)S(1)} %fusion.84), channel_id=2, replica_groups=mesh['chain'=8,'col'=4] {'chain'}, dimensions={0}, use_global_device_ids=true | all-gather | bytes 73728 | tf_op jit(solution)/shard_map/while/body/eval_jaxpr/all_gather | solution.py:63
  338.2 249.2 %while.36 = (s32[]{:T(128)}, f32[4,32,128]{2,0,1:T(4,128)S(1)}, bf16[4,32,128]{2,1,0:T(8,128)(2,1)S(1)}, s32[24]{0:T(128)S(1)}, s32[24]{0:T(128)S(1)}, /*index=5...) while((s32[]{:T(128)}, f32[4,32,128]{2,0,1:T(4,128)S(1)}, ...), condition=%wide.region_18.19_spmd.clone.clone, body=%wide.region_14.18_spmd.clone.clone.sunk | while | flops 31032652 | bytes 2840456 | solution.py:137
  341.7 5.2 all_gather.28
  347.7 30.5 %all-gather.7 = bf16[256,128]{1,0:T(8,128)(2,1)S(1)} all-gather(bf16[32,128]{1,0:T(8,128)(2,1)S(1)} %fusion.94), channel_id=3, replica_groups=mesh['chain'=8,'col'=4] {'chain'}, dimensions={0}, use_global_device_ids=true | all-gather | bytes 73728 | tf_op jit(solution)/shard_map/while/body/eval_jaxpr/all_gather | solution.py:120
  383.2 5.2 all_gather.28
  389.3 30.5 %all-gather.7 = bf16[256,128]{1,0:T(8,128)(2,1)S(1)} all-gather(bf16[32,128]{1,0:T(8,128)(2,1)S(1)} %fusion.94), channel_id=3, replica_groups=mesh['chain'=8,'col'=4] {'chain'}, dimensions={0}, use_global_device_ids=true | all-gather | bytes 73728 | tf_op jit(solution)/shard_map/while/body/eval_jaxpr/all_gather | solution.py:120
  430.8 30.5 %all-gather.7 = bf16[256,128]{1,0:T(8,128)(2,1)S(1)} all-gather(bf16[32,128]{1,0:T(8,128)(2,1)S(1)} %fusion.94), channel_id=3, replica_groups=mesh['chain'=8,'col'=4] {'chain'}, dimensions={0}, use_global_device_ids=true | all-gather | bytes 73728 | tf_op jit(solution)/shard_map/while/body/eval_jaxpr/all_gather | solution.py:120
  472.3 30.5 %all-gather.7 = bf16[256,128]{1,0:T(8,128)(2,1)S(1)} all-gather(bf16[32,128]{1,0:T(8,128)(2,1)S(1)} %fusion.94), channel_id=3, replica_groups=mesh['chain'=8,'col'=4] {'chain'}, dimensions={0}, use_global_device_ids=true | all-gather | bytes 73728 | tf_op jit(solution)/shard_map/while/body/eval_jaxpr/all_gather | solution.py:120
  513.8 30.5 %all-gather.7 = bf16[256,128]{1,0:T(8,128)(2,1)S(1)} all-gather(bf16[32,128]{1,0:T(8,128)(2,1)S(1)} %fusion.94), channel_id=3, replica_groups=mesh['chain'=8,'col'=4] {'chain'}, dimensions={0}, use_global_device_ids=true | all-gather | bytes 73728 | tf_op jit(solution)/shard_map/while/body/eval_jaxpr/all_gather | solution.py:120
  555.4 30.5 %all-gather.7 = bf16[256,128]{1,0:T(8,128)(2,1)S(1)} all-gather(bf16[32,128]{1,0:T(8,128)(2,1)S(1)} %fusion.94), channel_id=3, replica_groups=mesh['chain'=8,'col'=4] {'chain'}, dimensions={0}, use_global_device_ids=true | all-gather | bytes 73728 | tf_op jit(solution)/shard_map/while/body/eval_jaxpr/all_gather | solution.py:120
  (211 shorter events, 100.0 us)
Async XLA Ops:
  4.0 13.8 %all-to-all-start = ((s32[8,3,2]{1,2,0:T(2,128)}), s32[8,3,2]{1,2,0:T(2,128)S(1)}, u32[]{:S(2)}, u32[]{:S(2)}) async-start(s32[8,3,2]{1,2,0:T(2,128)} %copy.18), calls=%async_computation | async-start | bytes 16384 | tf_op jit(solution)/shard_map/all_to_all | solution.py:96
  17.8 5.3 copy-start.2
  17.8 320.4 %all-to-all-start.1 = ((bf16[8,3,128,128]{3,2,1,0:T(8,128)(2,1)}), bf16[8,3,128,128]{3,2,1,0:T(8,128)(2,1)S(1)}, u32[]{:S(2)}, u32[]{:S(2)}) async-start(bf16[8,3,128,128]{3,2,1,0:T(8,128)(2,1)} %bitcast.42), calls=%async_computation.1 | async-start | bytes 1572864 | tf_op jit(solution)/shard_map/all_to_all | solution.py:95
  587.4 0.6 copy-start
  587.4 0.6 copy-start.1
